TPU v7x, 32 devices: a whole 2x2x4 slice. The times are simulated.
32 devices in a mesh: mem: 8 (over y, x, core), lat: 4 (over z).
Axes of the slice: x: 2, y: 2, z: 4, core: 2. Of those that a mesh axis runs over, the one named last changes fastest.
Arguments:
- fields: float32 [1024, 32, 256], P('mem', 'lat'), may hold values from -8 to 8
- forcing: float32 [32, 256], P('lat'), may hold values from 2 to 8
- obs_cell: int32 [4, 32, 256], P('lat'), may hold values from 0 to 63
- obs_count: int32 [4, 32], P('lat', 'mem'), may hold values from 64 to 256, as said below
- obs_value: float32 [4, 32, 256], P('lat', 'mem'), may hold values from -12 to 12
- obs_var: float32 [4, 32, 256], P('lat', 'mem'), may hold values from 0.25 to 1
Outputs:
- analysis: float32 [1024, 32, 256], P('mem', 'lat')
Inputs may be any that keep to these rules, and one draw needn't show every extreme that they name: `obs_count`: each latitude strip has a patch with exactly 256 live observations.
All inputs are finite; a program needn't handle non-finite values.
Results may differ from a plain program's by a relative error of at most 0.0003.
Values sent between devices are 32-bit elements; how exact they have to be, the bound alone decides.
A program may use at most 64 MiB of HBM per device.

v0:
```python
import jax
import jax.numpy as jnp
from jax import lax
from jax.sharding import PartitionSpec as P

PATCH_CELLS = 64
STEPS = 4


TIME_STEP = 0.05
LAT_MIXING = 4.0


def with_halo(value, sides, width):
    for axis, dim in sides:
        size, length = (lax.axis_size(axis), value.shape[dim])
        up = [(i, (i + 1) % size) for i in range(size - 1)]
        down = [(j, i) for i, j in up]
        last = lax.slice_in_dim(value, length - width, length, axis=dim)
        leading = lax.slice_in_dim(value, 0, width, axis=dim)
        before = lax.ppermute(last, axis, up)
        after = lax.ppermute(leading, axis, down)
        value = jnp.concatenate([before, value, after], axis=dim)
    return value


def advance(middle, upper, lower, forcing):
    eastern = jnp.roll(middle, -1, axis=2)
    western = jnp.roll(middle, 1, axis=2)
    far_west = jnp.roll(middle, 2, axis=2)
    tendency = (
        (eastern - far_west) * western
        - middle
        + forcing
        + LAT_MIXING * (upper + lower - 2.0 * middle)
    )
    return middle + TIME_STEP * tendency


def analyse(patch_cells, observed, live_count, values, variances):
    members = patch_cells.shape[1]
    anomalies = patch_cells - jnp.mean(patch_cells, axis=1, keepdims=True)
    mean_obs = jnp.mean(observed, axis=1, keepdims=True)
    live = (jnp.arange(observed.shape[0]) < live_count)[:, None]
    obs_anom = jnp.where(live, observed - mean_obs, jnp.float32(0.0))
    gram = jnp.dot(obs_anom, obs_anom.T, precision=lax.Precision.HIGHEST) / (members - 1)
    gram = gram + jnp.diag(jnp.where(live[:, 0], variances, jnp.float32(1.0)))
    innovation = jnp.where(live, values[:, None] - mean_obs, jnp.float32(0.0))
    target = innovation - 0.5 * obs_anom
    factor = jnp.linalg.cholesky(gram)
    solved = jax.scipy.linalg.cho_solve((factor, True), target)
    cross = jnp.dot(anomalies, obs_anom.T, precision=lax.Precision.HIGHEST) / (members - 1)
    return patch_cells + jnp.dot(cross, solved, precision=lax.Precision.HIGHEST)


def local(fields, forcing, obs_cell, obs_count, obs_value, obs_var):
    group_size, rows_dev, lon_cells = fields.shape
    stacked = jnp.concatenate([fields, forcing[None]], axis=0)
    extended = with_halo(stacked, (("lat", 1),), STEPS)
    current = extended[:-1]
    row_forcing = extended[-1]
    for repeat_index in range(STEPS):
        updated = advance(current[:, 1:-1], current[:, 2:], current[:, :-2], row_forcing[1:-1])
        margin = STEPS - repeat_index - 1
        global_rows = lax.axis_index("lat") * rows_dev - margin + jnp.arange(updated.shape[1])
        inside = (global_rows >= 0) & (global_rows < lax.axis_size("lat") * rows_dev)
        current = jnp.where(inside[None, :, None], updated, jnp.float32(0.0))
        row_forcing = row_forcing[1:-1]
    strip_cells = rows_dev * lon_cells
    flat_fields = current.reshape(group_size, strip_cells)
    patch_dev = obs_count.shape[1]
    first_patch = lax.axis_index("mem") * patch_dev
    local_cells = lax.dynamic_slice_in_dim(obs_cell[0], first_patch, patch_dev, 0)
    gathered = lax.all_to_all(flat_fields, "mem", split_axis=1, concat_axis=0, tiled=True)
    members = gathered.shape[0]
    patches = gathered.T.reshape(patch_dev, PATCH_CELLS, members)
    observed = jax.vmap(lambda cells, index: jnp.take(cells, index, axis=0))(patches, local_cells)

    def one_patch(items):
        patch_cells, patch_observed, live_count, values, variances = items
        return analyse(patch_cells, patch_observed, live_count, values, variances)

    result = lax.map(one_patch, (patches, observed, obs_count[0], obs_value[0], obs_var[0]))
    outgoing = result.reshape(patch_dev * PATCH_CELLS, members).T
    returned = lax.all_to_all(outgoing, "mem", split_axis=0, concat_axis=1, tiled=True)
    return returned.reshape(group_size, rows_dev, lon_cells)


def solution(mesh):
    placed = (
        P("mem", "lat", None),
        P("lat", None),
        P("lat", None, None),
        P("lat", "mem"),
        P("lat", "mem", None),
        P("lat", "mem", None),
    )
    return jax.shard_map(
        local, mesh=mesh, in_specs=placed, out_specs=P("mem", "lat", None), check_vma=False
    )
```

profile of v0, /device:TPU:1, one launch (start us, length us, event | category | flops | bytes accessed | tf_op | source)
XLA Modules:
  0.0 395.3 jit_solution(14196573046717555120)
XLA Ops:
  4.2 4.7 %collective-permute-start = (f32[129,4,256]{2,1,0:T(4,128)S(1)}, f32[129,4,256]{2,1,0:T(4,128)S(1)}, u32[]{:S(2)}, u32[]{:S(2)}) collective-permute-start(f32[129,4,256]{2,1,0:T(4,128)S(1)} %copy.20), channel_id=1, source_target_pairs={{0,1},{1,2},{2,3},{4,5},{5,6},{6,7},{8,9},{9,10},{10,11},{12,13},{... | collective-permute-start | bytes 1585160 | tf_op jit(solution)/shard_map/ppermute | solution.py:21
  8.9 9.5 %collective-permute-done.1 = f32[129,4,256]{2,1,0:T(4,128)S(1)} collective-permute-done((f32[129,4,256]{2,1,0:T(4,128)S(1)}, f32[129,4,256]{2,1,0:T(4,128)S(1)}, u32[]{:S(2)}, u32[]{:S(2)}) %collective-permute-start.1) | collective-permute-done | bytes 528416 | tf_op jit(solution)/shard_map/ppermute | solution.py:22
  31.3 5.4 %all-to-all-start = ((f32[128,8,256]{2,0,1:T(8,128)}), f32[128,8,256]{2,0,1:T(8,128)S(1)}, u32[]{:S(2)}, u32[]{:S(2)}) async-start(f32[128,8,256]{2,0,1:T(8,128)} %fusion.69), calls=%async_computation | async-start | bytes 2097152 | tf_op jit(solution)/shard_map/all_to_all | solution.py:74
  38.1 10.5 %all-to-all-done = f32[128,8,256]{2,0,1:T(8,128)S(1)} async-done(((f32[128,8,256]{2,0,1:T(8,128)}), f32[128,8,256]{2,0,1:T(8,128)S(1)}, u32[]{:S(2)}, u32[]{:S(2)}) %all-to-all-start) | async-done | bytes 1048608 | tf_op jit(solution)/shard_map/all_to_all | solution.py:74
  49.0 14.9 %gather_fusion = f32[1024,1024]{1,0:T(8,128)} fusion(f32[4,64,1024]{2,1,0:T(8,128)S(1)} %bitcast.139, s32[1024]{0:T(1024)S(1)} %bitcast.141), kind=kCustom, calls=%fused_computation | custom fusion | bytes 8396800 | tf_op jit(solution)/shard_map/vmap(jit(_take))/gather | solution.py:77
  63.9 4.5 %broadcast_select_fusion.1 = f32[4,256,1024]{2,1,0:T(8,128)} fusion(f32[4,256,1024]{2,1,0:T(8,128)} %bitcast.143, pred[4,256]{1,0:T(4,128)(4,1)S(1)} %compare_and_fusion), kind=kLoop, calls=%fused_computation.75 | loop fusion | flops 1048576 | bytes 8389632 | tf_op jit(solution)/shard_map/vmap(jit(_take))/select_n | solution.py:77
  68.3 305.1 %while.13 = (s32[]{:T(128)}, f32[4,64,1024]{2,1,0:T(8,128)S(1)}, f32[4,64,1024]{2,1,0:T(8,128)S(1)}, s32[4]{0:T(128)S(1)}, f32[4,256,1024]{2,1,0:T(8,128)}, /*in...) while((s32[]{:T(128)}, f32[4,64,1024]{2,1,0:T(8,128)S(1)}, ...), condition=%wide.region_7.8_spmd, body=%wide.region_0.7_spmd.sunk | while | flops 2470348544 | bytes 18700148 | solution.py:83
  75.6 2.8 convolution_multiply_fusion.5
  78.6 11.7 %cholesky.184 = f32[128,128]{1,0:T(8,128)S(1)} custom-call(f32[128,128]{1,0:T(8,128)S(1)} %cholesky.183), custom_call_target="Cholesky" | custom-call | tf_op jit(solution)/shard_map/while/body/eval_jaxpr/jit(cholesky)/cholesky | solution.py:50
  91.0 9.8 %custom-call.27 = f32[1,128,128]{1,2,0:T(8,128)S(1)} custom-call(f32[1,128,128]{2,1,0:T(8,128)S(1)} %get-tuple-element.192), custom_call_target="InvertDiagBlocksLowerTriangular" | custom-call | tf_op jit(solution)/shard_map/while/body/eval_jaxpr/jit(cholesky)/cholesky | solution.py:50
  101.3 11.7 %cholesky.186 = f32[128,128]{1,0:T(8,128)S(1)} custom-call(f32[128,128]{1,0:T(8,128)S(1)} %convolution_subtract_fusion.6), custom_call_target="Cholesky" | custom-call | tf_op jit(solution)/shard_map/while/body/eval_jaxpr/jit(cholesky)/cholesky | solution.py:50
  115.0 3.9 while.14
  119.0 19.7 %custom-call.29 = f32[2,128,128]{1,2,0:T(8,128)S(1)} custom-call(f32[2,128,128]{2,1,0:T(8,128)S(1)} %get-tuple-element.198), custom_call_target="InvertDiagBlocksLowerTriangular" | custom-call | tf_op jit(solution)/shard_map/while/body/eval_jaxpr/jit(_cho_solve)/triangular_solve | solution.py:51
  151.8 2.9 convolution_multiply_fusion.5
  155.0 11.7 %cholesky.184 = f32[128,128]{1,0:T(8,128)S(1)} custom-call(f32[128,128]{1,0:T(8,128)S(1)} %cholesky.183), custom_call_target="Cholesky" | custom-call | tf_op jit(solution)/shard_map/while/body/eval_jaxpr/jit(cholesky)/cholesky | solution.py:50
  167.4 9.8 %custom-call.27 = f32[1,128,128]{1,2,0:T(8,128)S(1)} custom-call(f32[1,128,128]{2,1,0:T(8,128)S(1)} %get-tuple-element.192), custom_call_target="InvertDiagBlocksLowerTriangular" | custom-call | tf_op jit(solution)/shard_map/while/body/eval_jaxpr/jit(cholesky)/cholesky | solution.py:50
  177.7 11.7 %cholesky.186 = f32[128,128]{1,0:T(8,128)S(1)} custom-call(f32[128,128]{1,0:T(8,128)S(1)} %convolution_subtract_fusion.6), custom_call_target="Cholesky" | custom-call | tf_op jit(solution)/shard_map/while/body/eval_jaxpr/jit(cholesky)/cholesky | solution.py:50
  191.4 3.9 while.14
  195.3 19.7 %custom-call.29 = f32[2,128,128]{1,2,0:T(8,128)S(1)} custom-call(f32[2,128,128]{2,1,0:T(8,128)S(1)} %get-tuple-element.198), custom_call_target="InvertDiagBlocksLowerTriangular" | custom-call | tf_op jit(solution)/shard_map/while/body/eval_jaxpr/jit(_cho_solve)/triangular_solve | solution.py:51
  228.2 2.8 convolution_multiply_fusion.5
  231.3 11.7 %cholesky.184 = f32[128,128]{1,0:T(8,128)S(1)} custom-call(f32[128,128]{1,0:T(8,128)S(1)} %cholesky.183), custom_call_target="Cholesky" | custom-call | tf_op jit(solution)/shard_map/while/body/eval_jaxpr/jit(cholesky)/cholesky | solution.py:50
  243.7 9.8 %custom-call.27 = f32[1,128,128]{1,2,0:T(8,128)S(1)} custom-call(f32[1,128,128]{2,1,0:T(8,128)S(1)} %get-tuple-element.192), custom_call_target="InvertDiagBlocksLowerTriangular" | custom-call | tf_op jit(solution)/shard_map/while/body/eval_jaxpr/jit(cholesky)/cholesky | solution.py:50
  254.0 11.7 %cholesky.186 = f32[128,128]{1,0:T(8,128)S(1)} custom-call(f32[128,128]{1,0:T(8,128)S(1)} %convolution_subtract_fusion.6), custom_call_target="Cholesky" | custom-call | tf_op jit(solution)/shard_map/while/body/eval_jaxpr/jit(cholesky)/cholesky | solution.py:50
  267.7 3.9 while.14
  271.6 19.7 %custom-call.29 = f32[2,128,128]{1,2,0:T(8,128)S(1)} custom-call(f32[2,128,128]{2,1,0:T(8,128)S(1)} %get-tuple-element.198), custom_call_target="InvertDiagBlocksLowerTriangular" | custom-call | tf_op jit(solution)/shard_map/while/body/eval_jaxpr/jit(_cho_solve)/triangular_solve | solution.py:51
  304.5 2.8 convolution_multiply_fusion.5
  307.5 11.7 %cholesky.184 = f32[128,128]{1,0:T(8,128)S(1)} custom-call(f32[128,128]{1,0:T(8,128)S(1)} %cholesky.183), custom_call_target="Cholesky" | custom-call | tf_op jit(solution)/shard_map/while/body/eval_jaxpr/jit(cholesky)/cholesky | solution.py:50
  319.9 9.8 %custom-call.27 = f32[1,128,128]{1,2,0:T(8,128)S(1)} custom-call(f32[1,128,128]{2,1,0:T(8,128)S(1)} %get-tuple-element.192), custom_call_target="InvertDiagBlocksLowerTriangular" | custom-call | tf_op jit(solution)/shard_map/while/body/eval_jaxpr/jit(cholesky)/cholesky | solution.py:50
  330.2 11.7 %cholesky.186 = f32[128,128]{1,0:T(8,128)S(1)} custom-call(f32[128,128]{1,0:T(8,128)S(1)} %convolution_subtract_fusion.6), custom_call_target="Cholesky" | custom-call | tf_op jit(solution)/shard_map/while/body/eval_jaxpr/jit(cholesky)/cholesky | solution.py:50
  343.9 3.9 while.14
  347.8 19.7 %custom-call.29 = f32[2,128,128]{1,2,0:T(8,128)S(1)} custom-call(f32[2,128,128]{2,1,0:T(8,128)S(1)} %get-tuple-element.198), custom_call_target="InvertDiagBlocksLowerTriangular" | custom-call | tf_op jit(solution)/shard_map/while/body/eval_jaxpr/jit(_cho_solve)/triangular_solve | solution.py:51
  373.8 19.9 %all_to_all.32 = f32[8,128,256]{2,1,0:T(8,128)S(1)} all-to-all(f32[8,128,256]{2,1,0:T(8,128)S(1)} %bitcast.145), channel_id=1, replica_groups=mesh['mem'=8,'lat'=4] {'mem'}, dimensions={0} | all-to-all | bytes 2097152 | tf_op jit(solution)/shard_map/all_to_all | solution.py:85
  (200 shorter events, 96.7 us)
Async XLA Ops:
  2.7 15.7 %collective-permute-start.1 = (f32[129,4,256]{2,1,0:T(4,128)S(1)}, f32[129,4,256]{2,1,0:T(4,128)S(1)}, u32[]{:S(2)}, u32[]{:S(2)}) collective-permute-start(f32[129,4,256]{2,1,0:T(4,128)S(1)} %copy.21), channel_id=1, source_target_pairs={{1,0},{2,1},{3,2},{5,4},{6,5},{7,6},{9,8},{10,9},{11,10},{13,12},{... | collective-permute-start | bytes 1585160 | tf_op jit(solution)/shard_map/ppermute | solution.py:22
  4.2 15.3 %collective-permute-start = (f32[129,4,256]{2,1,0:T(4,128)S(1)}, f32[129,4,256]{2,1,0:T(4,128)S(1)}, u32[]{:S(2)}, u32[]{:S(2)}) collective-permute-start(f32[129,4,256]{2,1,0:T(4,128)S(1)} %copy.20), channel_id=1, source_target_pairs={{0,1},{1,2},{2,3},{4,5},{5,6},{6,7},{8,9},{9,10},{10,11},{12,13},{... | collective-permute-start | bytes 1585160 | tf_op jit(solution)/shard_map/ppermute | solution.py:21
  28.6 0.7 copy-start
  31.3 17.4 %all-to-all-start = ((f32[128,8,256]{2,0,1:T(8,128)}), f32[128,8,256]{2,0,1:T(8,128)S(1)}, u32[]{:S(2)}, u32[]{:S(2)}) async-start(f32[128,8,256]{2,0,1:T(8,128)} %fusion.69), calls=%async_computation | async-start | bytes 2097152 | tf_op jit(solution)/shard_map/all_to_all | solution.py:74
  63.9 4.5 %copy-start.1 = (s32[1,4]{1,0:T(1,128)S(1)}, s32[1,4]{1,0:T(1,128)}, u32[]{:S(2)}) copy-start(s32[1,4]{1,0:T(1,128)} %param.11) | copy-start | bytes 52
where the time goes:
time: 398 us; the launch traced here: 395 us
  other arithmetic  250 us (63%)
  local copies, waits for them, and re-layouts  46.7 us (12%)
  matrix products  40.3 us (10%)
  waiting for transfers between devices  21 us (5%)
  blocking collectives  19.9 us (5%)
  starting transfers between devices  11.4 us (3%)
  loops' own time  6 us (2%)
    another operation x28, other arithmetic, analyse(): factor = jnp.linalg.cholesky(gram)  138 us
    another operation x12, other arithmetic, analyse(): solved = jax.scipy.linalg.cho_solve((factor, True), target)  78.8 us
    all_to_all x1, blocking collectives, local(): lax.all_to_all(outgoing, 'mem', split_axis=0, concat_axis=1, tiled=True)  19.9 us
    another operation x24, local copies, waits for them, and re-layouts  15.6 us
    gather x1, local copies, waits for them, and re-layouts, local(): jnp.take(cells, index, axis=0)  14.9 us
    another operation x24, matrix products, analyse(): solved = jax.scipy.linalg.cho_solve((factor, True), target)  14.5 us
    dot_general x4, matrix products, analyse(): jnp.dot(obs_anom, obs_anom.T, precision=lax.Precision.HIGHEST)  11.3 us
    all_to_all x1, waiting for transfers between devices, local(): lax.all_to_all(flat_fields, 'mem', split_axis=1, concat_axis=0, tiled=True)  10.5 us
  transfers between devices with their start and end apart: 3, of which 3 were waited for; matrix products, arithmetic and copies ran while one was open for 0% of the time, Pallas kernels for 0%

commit v1 on v0

v1 whole, which is shorter than its diff:
```python
import functools

import jax
import jax.numpy as jnp
from jax import lax
from jax.experimental import pallas as pl
from jax.experimental.pallas import tpu as pltpu
from jax.sharding import PartitionSpec as P

PATCH_CELLS = 64
STEPS = 4
TIME_STEP = 0.05
LAT_MIXING = 4.0
HALO_CHUNKS = 4
TILE = 8

MESH = pl.DeviceIdType.MESH
HIGHEST = lax.Precision.HIGHEST


def lane_group(shape):
    return lax.broadcasted_iota(jnp.int32, shape, 1) // PATCH_CELLS


def diagonal_blocks(square):
    lon = square.shape[1]
    groups = lane_group((PATCH_CELLS, lon))
    total = jnp.zeros((PATCH_CELLS, lon), jnp.float32)
    for q in range(lon // PATCH_CELLS):
        block = square[q * PATCH_CELLS:(q + 1) * PATCH_CELLS]
        total = jnp.where(groups == q, block, total)
    return total


def block_diagonal(blocks):
    lon = blocks.shape[1]
    groups = lane_group(blocks.shape)
    return jnp.concatenate(
        [jnp.where(groups == q, blocks, 0.0) for q in range(lon // PATCH_CELLS)], axis=0
    )


def as_column(row, eye, groups):
    spread = jnp.where(eye, jnp.broadcast_to(row, eye.shape), 0.0)
    total = jnp.zeros(eye.shape, jnp.float32)
    for q in range(eye.shape[1] // PATCH_CELLS):
        column = jnp.sum(jnp.where(groups == q, spread, 0.0), axis=1, keepdims=True)
        total = jnp.where(groups == q, column, total)
    return total


def invert(blocks, in_group):
    lon = blocks.shape[1]
    sublane = lax.broadcasted_iota(jnp.int32, (PATCH_CELLS, 128), 0)
    lane = lax.broadcasted_iota(jnp.int32, (PATCH_CELLS, 128), 1)
    start = (lane // PATCH_CELLS) * PATCH_CELLS
    position = lane - start
    halves = [blocks[:, h * 128:(h + 1) * 128] for h in range(lon // 128)]
    for k in range(PATCH_CELLS):
        at_k = position == k
        on_row = sublane == k
        source = start + k
        updated = []
        for half in halves:
            column = jnp.take_along_axis(half, source, axis=1, mode="promise_in_bounds")
            inverse = 1.0 / column[k:k + 1]
            row = jnp.where(at_k[k:k + 1], 1.0, half[k:k + 1]) * inverse
            base = jnp.where(at_k | on_row, 0.0, half)
            factor = jnp.where(on_row, -1.0, column)
            updated.append(base - factor * row)
        halves = updated
    return jnp.concatenate(halves, axis=1)


def kernel(n_mem, n_lat, fields_ref, forcing_ref, cell_ref, count_ref, value_ref, var_ref, out_ref,
           ext, cur, fbuf, fwide, gsend, grecv, nsend, nrecv,
           halo_send, halo_recv, force_send, force_recv, gram_send, gram_recv, gain_send, gain_recv):
    rows, members, lon = cur.shape
    share = n_mem // rows
    per_row = lon // PATCH_CELLS
    chunk = members // HALO_CHUNKS
    me = lax.axis_index("mem")
    strip = lax.axis_index("lat")
    has_before = strip > 0
    has_after = strip < n_lat - 1
    my_row = me // share
    solver = lax.rem(me, share) == 0

    barrier = pltpu.get_barrier_semaphore()
    for d in range(1, n_mem):
        pl.semaphore_signal(barrier, inc=1, device_id={"mem": lax.rem(me + d, n_mem)}, device_id_type=MESH)

    @pl.when(has_before)
    def _():
        pl.semaphore_signal(barrier, inc=1, device_id={"lat": strip - 1}, device_id_type=MESH)

    @pl.when(has_after)
    def _():
        pl.semaphore_signal(barrier, inc=1, device_id={"lat": strip + 1}, device_id_type=MESH)

    for r in range(rows):
        for h in range(lon // 128):
            ext[STEPS + r, :, h * 128:(h + 1) * 128] = fields_ref[
                pl.ds(h * rows + r, members, stride=rows * (lon // 128)), :]

    @pl.when(jnp.logical_not(has_before))
    def _():
        ext[0:STEPS] = jnp.zeros((STEPS, members, lon), jnp.float32)
        fbuf[0] = jnp.zeros((rows, lon), jnp.float32)

    @pl.when(jnp.logical_not(has_after))
    def _():
        ext[STEPS + rows:] = jnp.zeros((STEPS, members, lon), jnp.float32)
        fbuf[1] = jnp.zeros((rows, lon), jnp.float32)

    pl.semaphore_wait(barrier, n_mem - 1 + has_before.astype(jnp.int32) + has_after.astype(jnp.int32))

    def halo_copy(side, c):
        span = pl.ds(c * chunk, chunk)
        source, target = ((rows, 0), (STEPS, STEPS + rows))[side]
        return pltpu.make_async_remote_copy(
            src_ref=ext.at[pl.ds(source, STEPS), span],
            dst_ref=ext.at[pl.ds(target, STEPS), span],
            send_sem=halo_send.at[side, c],
            recv_sem=halo_recv.at[side, c],
            device_id={"lat": (strip + 1, strip - 1)[side]},
            device_id_type=MESH,
        )

    def force_copy(side):
        return pltpu.make_async_remote_copy(
            src_ref=forcing_ref,
            dst_ref=fbuf.at[side],
            send_sem=force_send.at[side],
            recv_sem=force_recv.at[side],
            device_id={"lat": (strip + 1, strip - 1)[side]},
            device_id_type=MESH,
        )

    can_send = (has_after, has_before)
    can_receive = (has_before, has_after)
    for side in range(2):
        @pl.when(can_send[side])
        def _(side=side):
            force_copy(side).start()
    for c in range(HALO_CHUNKS):
        for side in range(2):
            @pl.when(can_send[side])
            def _(side=side, c=c):
                halo_copy(side, c).start()

    cell_of = lax.broadcasted_iota(jnp.int32, (PATCH_CELLS, cell_ref.shape[1]), 0)
    slot = lax.broadcasted_iota(jnp.int32, (1, cell_ref.shape[1]), 1)
    groups = lane_group((PATCH_CELLS, lon))
    weight = jnp.zeros((PATCH_CELLS, lon), jnp.float32)
    pull = jnp.zeros((PATCH_CELLS, lon), jnp.float32)
    for q in range(per_row):
        cells = cell_ref[pl.ds(my_row * per_row + q, 1), :]
        precision = jnp.where(slot < count_ref[0, q], 1.0 / var_ref[q:q + 1, :], 0.0)
        hit = cell_of == cells
        w = jnp.sum(jnp.where(hit, precision, 0.0), axis=1, keepdims=True)
        b = jnp.sum(jnp.where(hit, precision * value_ref[q:q + 1, :], 0.0), axis=1, keepdims=True)
        weight = jnp.where(groups == q, w, weight)
        pull = jnp.where(groups == q, b, pull)

    for side in range(2):
        @pl.when(can_receive[side])
        def _(side=side):
            force_copy(side).wait_recv()
    own = forcing_ref[...]
    for i in range(2 * STEPS + rows):
        if i < STEPS:
            line = fbuf[0, rows - STEPS + i:rows - STEPS + i + 1, :]
        elif i < STEPS + rows:
            line = own[i - STEPS:i - STEPS + 1]
        else:
            line = fbuf[1, i - STEPS - rows:i - STEPS - rows + 1, :]
        fwide[i] = jnp.broadcast_to(line * TIME_STEP, (TILE, lon))

    def advance(u, upper, lower, force):
        eastern = pltpu.roll(u, lon - 1, 1)
        western = pltpu.roll(u, 1, 1)
        far_west = pltpu.roll(u, 2, 1)
        tendency = (eastern - far_west) * western - u + LAT_MIXING * (upper + lower - 2.0 * u)
        return u + (TIME_STEP * tendency + force)

    def forecast(start):
        span = pl.ds(pl.multiple_of(start, TILE), TILE)
        state = [ext[i, span, :] for i in range(2 * STEPS + rows)]
        for step in range(STEPS):
            lo = step + 1
            fresh = []
            for i in range(lo, 2 * STEPS + rows - lo):
                at = i - step
                moved = advance(state[at], state[at + 1], state[at - 1], fwide[i])
                if i < STEPS:
                    moved = jnp.where(has_before, moved, 0.0)
                elif i >= STEPS + rows:
                    moved = jnp.where(has_after, moved, 0.0)
                fresh.append(moved)
            state = fresh
        for r in range(rows):
            cur[r, span, :] = state[r]

    for c in range(HALO_CHUNKS):
        for side in range(2):
            @pl.when(can_receive[side])
            def _(side=side, c=c):
                halo_copy(side, c).wait_recv()

        @pl.loop(0, chunk // TILE)
        def _(i, c=c):
            forecast(c * chunk + i * TILE)

    def gram_copy(d):
        target = lax.rem(me + d, n_mem)
        return pltpu.make_async_remote_copy(
            src_ref=gsend.at[target // share],
            dst_ref=grecv.at[d - 1],
            send_sem=gram_send.at[d - 1],
            recv_sem=gram_recv.at[d - 1],
            device_id={"mem": target},
            device_id_type=MESH,
        )

    def moments(row):
        values = cur[row]
        mean = jnp.sum(values, axis=0, keepdims=True) * (1.0 / members)
        centred = values - mean
        square = lax.dot_general(
            centred, centred, (((0,), (0,)), ((), ())), precision=HIGHEST,
            preferred_element_type=jnp.float32,
        )
        gsend[row, 0:PATCH_CELLS, :] = diagonal_blocks(square)
        gsend[row, PATCH_CELLS:, :] = jnp.broadcast_to(mean, (TILE, lon))

    @pl.loop(1, n_mem)
    def _(d):
        target = lax.rem(me + d, n_mem)

        @pl.when(lax.rem(target, share) == 0)
        def _():
            moments(target // share)
            gram_copy(d).start()

    def gain_copy(d):
        return pltpu.make_async_remote_copy(
            src_ref=nsend,
            dst_ref=nrecv.at[my_row],
            send_sem=gain_send.at[d - 1],
            recv_sem=gain_recv.at[d - 1],
            device_id={"mem": lax.rem(me + d, n_mem)},
            device_id_type=MESH,
        )

    def apply(row, gain_ref):
        mean = gain_ref[PATCH_CELLS:PATCH_CELLS + 1, :]
        shift = gain_ref[PATCH_CELLS + 1:PATCH_CELLS + 2, :]
        half = 0.5 * (cur[row] - mean)
        moved = jnp.dot(half, block_diagonal(gain_ref[0:PATCH_CELLS, :]), precision=HIGHEST,
                        preferred_element_type=jnp.float32)
        result = half + moved + (mean + shift)
        for h in range(lon // 128):
            out_ref[pl.ds(h * rows + row, members, stride=rows * (lon // 128)), :] = result[:, h * 128:(h + 1) * 128]

    @pl.when(solver)
    def _():
        moments(my_row)
        total = gsend[my_row, 0:PATCH_CELLS, :]
        means = [gsend[my_row, PATCH_CELLS:, :]]
        for d in range(1, n_mem):
            gram_copy(d).wait_recv()
            total = total + grecv[d - 1, 0:PATCH_CELLS, :]
            means.append(grecv[d - 1, PATCH_CELLS:, :])
        mean = functools.reduce(lambda a, b: a + b, means)[0:1] * (1.0 / n_mem)
        drift = jnp.concatenate([m[0:1] - mean for m in means], axis=0)
        spread = lax.dot_general(
            drift, drift, (((0,), (0,)), ((), ())), precision=HIGHEST, preferred_element_type=jnp.float32
        )
        cov = (total + members * diagonal_blocks(spread)) * (1.0 / (members * n_mem - 1))

        in_group = lax.broadcasted_iota(jnp.int32, (PATCH_CELLS, lon), 1) - groups * PATCH_CELLS
        eye = lax.broadcasted_iota(jnp.int32, (PATCH_CELLS, lon), 0) == in_group
        inverse = invert(jnp.where(eye, 1.0, 0.0) + weight * cov, in_group)
        misfit = pull - weight * as_column(mean, eye, groups)
        push = jnp.sum(misfit * cov, axis=0, keepdims=True)
        shift = jnp.sum(as_column(push, eye, groups) * inverse, axis=0, keepdims=True)
        nsend[0:PATCH_CELLS, :] = inverse
        first = lax.broadcasted_iota(jnp.int32, (TILE, lon), 0) == 0
        nsend[PATCH_CELLS:, :] = jnp.where(first, mean, shift)
        for d in range(1, n_mem):
            gain_copy(d).start()
        apply(my_row, nsend)

    @pl.loop(1, n_mem)
    def _(d):
        origin = lax.rem(me + n_mem - d, n_mem)

        @pl.when(lax.rem(origin, share) == 0)
        def _():
            gain_copy(d).wait_recv()
            apply(origin // share, nrecv.at[origin // share])

    for side in range(2):
        @pl.when(can_send[side])
        def _(side=side):
            force_copy(side).wait_send()
            for c in range(HALO_CHUNKS):
                halo_copy(side, c).wait_send()

    @pl.loop(1, n_mem)
    def _(d):
        @pl.when(lax.rem(lax.rem(me + d, n_mem), share) == 0)
        def _():
            gram_copy(d).wait_send()

        @pl.when(solver)
        def _():
            gain_copy(d).wait_send()


def local(n_mem, n_lat, fields, forcing, obs_cell, obs_count, obs_value, obs_var):
    members, rows, lon = fields.shape
    slots = obs_cell.shape[2]
    per_row = lon // PATCH_CELLS
    if obs_count.shape[1] != per_row:
        row = lax.axis_index("mem") // (n_mem // rows)
        obs_count, obs_value, obs_var = (
            lax.dynamic_slice_in_dim(lax.all_gather(a, "mem", axis=1, tiled=True), row * per_row, per_row, 1)
            for a in (obs_count, obs_value, obs_var)
        )
    block = PATCH_CELLS + TILE
    vmem = pl.BlockSpec(memory_space=pltpu.VMEM)
    dma = pltpu.SemaphoreType.DMA
    out = pl.pallas_call(
        functools.partial(kernel, n_mem, n_lat),
        out_shape=jax.ShapeDtypeStruct((members * rows * (lon // 128), 128), jnp.float32),
        in_specs=[vmem, vmem, vmem, pl.BlockSpec(memory_space=pltpu.SMEM), vmem, vmem],
        out_specs=vmem,
        scratch_shapes=[
            pltpu.VMEM((rows + 2 * STEPS, members, lon), jnp.float32),
            pltpu.VMEM((rows, members, lon), jnp.float32),
            pltpu.VMEM((2, rows, lon), jnp.float32),
            pltpu.VMEM((rows + 2 * STEPS, TILE, lon), jnp.float32),
            pltpu.VMEM((rows, block, lon), jnp.float32),
            pltpu.VMEM((n_mem - 1, block, lon), jnp.float32),
            pltpu.VMEM((block, lon), jnp.float32),
            pltpu.VMEM((rows, block, lon), jnp.float32),
            dma((2, HALO_CHUNKS)), dma((2, HALO_CHUNKS)),
            dma((2,)), dma((2,)),
            dma((n_mem - 1,)), dma((n_mem - 1,)),
            dma((n_mem - 1,)), dma((n_mem - 1,)),
        ],
        compiler_params=pltpu.CompilerParams(collective_id=0, has_side_effects=True),
        name="cycle",
    )(
        fields.reshape(members, rows, lon // 128, 128).transpose(0, 2, 1, 3).reshape(-1, 128),
        forcing,
        obs_cell.reshape(-1, slots),
        obs_count,
        obs_value.reshape(-1, slots),
        obs_var.reshape(-1, slots),
    )
    return out.reshape(members, lon // 128, rows, 128).transpose(0, 2, 1, 3).reshape(members, rows, lon)


def solution(mesh):
    placed = (
        P("mem", "lat", None),
        P("lat", None),
        P("lat", None, None),
        P("lat", "mem"),
        P("lat", "mem", None),
        P("lat", "mem", None),
    )
    return jax.shard_map(
        functools.partial(local, mesh.shape["mem"], mesh.shape["lat"]),
        mesh=mesh, in_specs=placed, out_specs=P("mem", "lat", None), check_vma=False,
    )
```

time: 398 us -> 47.6 us (0.12)
  other arithmetic: 250 us -> 0 us
  Pallas kernels: 0 us -> 45.2 us
  local copies, waits for them, and re-layouts: 46.7 us -> 2.26 us
  matrix products: 40.3 us -> 0 us
  waiting for transfers between devices: 21 us -> 0 us
  blocking collectives: 19.9 us -> 0 us
  starting transfers between devices: 11.4 us -> 0 us
  loops' own time: 6 us -> 0 us
    another operation x40 -> x0, other arithmetic: 217 us -> none  [the longest x28 138 us: analyse(): factor = jnp.linalg.cholesky(gram)]
    pallas_call x0 -> x1, Pallas kernels: none -> 45.2 us  [local(): pl.pallas_call(functools.partial(kernel, n_mem, n_lat), out_shape=jax.Sha...]
    dot_general x12 -> x0, matrix products: 23.9 us -> none  [the longest x4 11.3 us: analyse(): jnp.dot(obs_anom, obs_anom.T, precision=lax.Precision.HIGHEST)]
    all_to_all x1 -> x0, blocking collectives: 19.9 us -> none  [local(): lax.all_to_all(outgoing, 'mem', split_axis=0, concat_axis=1, tiled=True)]
    another operation x32 -> x0, matrix products: 16.4 us -> none  [the longest x24 14.5 us: analyse(): solved = jax.scipy.linalg.cho_solve((factor, True), target)]
    select_n x13 -> x0, other arithmetic: 16.1 us -> none  [the longest x4 6.43 us: local(): current = jnp.where(inside[None, :, None], updated, jnp.float32(0.0))]
    another operation x36 -> x0, local copies, waits for them, and re-layouts: 15.9 us -> none
    gather x1 -> x0, local copies, waits for them, and re-layouts: 14.9 us -> none  [local(): jnp.take(cells, index, axis=0)]
  transfers between devices with their start and end apart: 3 -> 0, of which waited for: 3 -> 0; matrix products, arithmetic and copies ran while one was open for 0% -> 0% of each run, Pallas kernels for 0% -> 0%
where the time goes in v1:
time: 47.6 us; the launch traced here: 47.5 us
  Pallas kernels  45.2 us (95%)
  local copies, waits for them, and re-layouts  2.26 us (5%)
    pallas_call x1, Pallas kernels, local(): pl.pallas_call(functools.partial(kernel, n_mem, n_lat), out_shape=jax.Sha...  45.2 us
    unnamed x1, local copies, waits for them, and re-layouts  2.26 us

profile of v1, /device:TPU:1, one launch (start us, length us, event | category | flops | bytes accessed | tf_op | source)
XLA Modules:
  0.0 47.5 jit_solution(14197864354924578916)
XLA Ops:
  0.0 45.2 %cycle.1 = f32[2048,128]{1,0:T(8,128)} custom-call(f32[2048,128]{1,0:T(8,128)} %bitcast.14, f32[8,256]{1,0:T(8,128)} %forcing_ref.1, s32[32,256]{1,0:T(8,128)} %bitcast.15, s32[1,4]{1,0:T(1,128)} %count_ref.1, f32[4,256]{1,0:T(4,128)} %bitcast.16, f32[4,256]{1,0:T(4,128)} %bitcast.17), custom_call_target="tpu_custom_call" | custom-call | tf_op jit(solution)/shard_map/cycle/pallas_call | solution.py:335
  45.2 2.3 %copy.8 = f32[128,8,256]{2,1,0:T(8,128)} copy(f32[128,8,256]{2,1,0:T(8,128)} %bitcast.13) | data formatting | bytes 2097152

commit v2 on v1

--- a/solution.py
+++ b/solution.py
@@ -13,6 +13,7 @@
 LAT_MIXING = 4.0
 HALO_CHUNKS = 4
 TILE = 8
+PIVOTS = 4
 
 MESH = pl.DeviceIdType.MESH
 HIGHEST = lax.Precision.HIGHEST
@@ -49,32 +50,59 @@
     return total
 
 
-def invert(blocks, in_group):
+def invert(blocks):
     lon = blocks.shape[1]
     sublane = lax.broadcasted_iota(jnp.int32, (PATCH_CELLS, 128), 0)
     lane = lax.broadcasted_iota(jnp.int32, (PATCH_CELLS, 128), 1)
     start = (lane // PATCH_CELLS) * PATCH_CELLS
     position = lane - start
     halves = [blocks[:, h * 128:(h + 1) * 128] for h in range(lon // 128)]
-    for k in range(PATCH_CELLS):
-        at_k = position == k
-        on_row = sublane == k
-        source = start + k
+    span = range(PIVOTS)
+    for k in range(0, PATCH_CELLS, PIVOTS):
+        in_columns = (position >= k) & (position < k + PIVOTS)
+        in_rows = (sublane >= k) & (sublane < k + PIVOTS)
         updated = []
         for half in halves:
-            column = jnp.take_along_axis(half, source, axis=1, mode="promise_in_bounds")
-            inverse = 1.0 / column[k:k + 1]
-            row = jnp.where(at_k[k:k + 1], 1.0, half[k:k + 1]) * inverse
-            base = jnp.where(at_k | on_row, 0.0, half)
-            factor = jnp.where(on_row, -1.0, column)
-            updated.append(base - factor * row)
+            columns = [
+                jnp.take_along_axis(half, start + (k + j), axis=1, mode="promise_in_bounds") for j in span
+            ]
+            small = [[columns[j][k + i:k + i + 1] for j in span] for i in span]
+            rows = [
+                jnp.where(
+                    in_columns[0:1],
+                    jnp.where(position[0:1] == k + i, 1.0, 0.0),
+                    half[k + i:k + i + 1],
+                )
+                for i in span
+            ]
+            for i in span:
+                inverse = 1.0 / small[i][i]
+                rows[i] = rows[i] * inverse
+                for j in range(i + 1, PIVOTS):
+                    small[i][j] = small[i][j] * inverse
+                for other in span:
+                    if other != i:
+                        factor = small[other][i]
+                        rows[other] = rows[other] - factor * rows[i]
+                        for j in range(i + 1, PIVOTS):
+                            small[other][j] = small[other][j] - factor * small[i][j]
+            fresh = jnp.where(in_columns | in_rows, 0.0, half)
+            for j in span:
+                factor = jnp.where(in_rows, jnp.where(sublane == k + j, -1.0, 0.0), columns[j])
+                fresh = fresh - factor * rows[j]
+            updated.append(fresh)
         halves = updated
     return jnp.concatenate(halves, axis=1)
 
 
+def split(values):
+    high = values.astype(jnp.bfloat16)
+    return high, (values - high.astype(jnp.float32)).astype(jnp.bfloat16)
+
+
 def kernel(n_mem, n_lat, fields_ref, forcing_ref, cell_ref, count_ref, value_ref, var_ref, out_ref,
-           ext, cur, fbuf, fwide, gsend, grecv, nsend, nrecv,
-           halo_send, halo_recv, force_send, force_recv, gram_send, gram_recv, gain_send, gain_recv):
+           landed, ext, cur, fbuf, fwide, gsend, grecv, nsend, nrecv,
+           load_sem, halo_send, halo_recv, force_send, force_recv, gram_send, gram_recv, gain_send, gain_recv):
     rows, members, lon = cur.shape
     share = n_mem // rows
     per_row = lon // PATCH_CELLS
@@ -98,21 +126,23 @@
     def _():
         pl.semaphore_signal(barrier, inc=1, device_id={"lat": strip + 1}, device_id_type=MESH)
 
-    for r in range(rows):
-        for h in range(lon // 128):
-            ext[STEPS + r, :, h * 128:(h + 1) * 128] = fields_ref[
-                pl.ds(h * rows + r, members, stride=rows * (lon // 128)), :]
-
-    @pl.when(jnp.logical_not(has_before))
-    def _():
-        ext[0:STEPS] = jnp.zeros((STEPS, members, lon), jnp.float32)
-        fbuf[0] = jnp.zeros((rows, lon), jnp.float32)
-
-    @pl.when(jnp.logical_not(has_after))
-    def _():
-        ext[STEPS + rows:] = jnp.zeros((STEPS, members, lon), jnp.float32)
-        fbuf[1] = jnp.zeros((rows, lon), jnp.float32)
-
+    pitch = rows * (lon // 128)
+
+    def load(c):
+        span = pl.ds(c * chunk * pitch, chunk * pitch)
+        return pltpu.make_async_copy(fields_ref.at[span], landed.at[span], load_sem.at[c])
+
+    for c in range(HALO_CHUNKS):
+        load(c).start()
+
+    def rows_first(c):
+        load(c).wait()
+        for r in range(rows):
+            for h in range(lon // 128):
+                ext[STEPS + r, c * chunk:(c + 1) * chunk, h * 128:(h + 1) * 128] = landed[
+                    pl.ds(c * chunk * pitch + h * rows + r, chunk, stride=pitch), :]
+
+    rows_first(0)
     pl.semaphore_wait(barrier, n_mem - 1 + has_before.astype(jnp.int32) + has_after.astype(jnp.int32))
 
     def halo_copy(side, c):
@@ -144,10 +174,22 @@
         def _(side=side):
             force_copy(side).start()
     for c in range(HALO_CHUNKS):
+        if c:
+            rows_first(c)
         for side in range(2):
             @pl.when(can_send[side])
             def _(side=side, c=c):
                 halo_copy(side, c).start()
+
+    @pl.when(jnp.logical_not(has_before))
+    def _():
+        ext[0:STEPS] = jnp.zeros((STEPS, members, lon), jnp.float32)
+        fbuf[0] = jnp.zeros((rows, lon), jnp.float32)
+
+    @pl.when(jnp.logical_not(has_after))
+    def _():
+        ext[STEPS + rows:] = jnp.zeros((STEPS, members, lon), jnp.float32)
+        fbuf[1] = jnp.zeros((rows, lon), jnp.float32)
 
     cell_of = lax.broadcasted_iota(jnp.int32, (PATCH_CELLS, cell_ref.shape[1]), 0)
     slot = lax.broadcasted_iota(jnp.int32, (1, cell_ref.shape[1]), 1)
@@ -226,10 +268,10 @@
     def moments(row):
         values = cur[row]
         mean = jnp.sum(values, axis=0, keepdims=True) * (1.0 / members)
-        centred = values - mean
+        high, low = split(values - mean)
         square = lax.dot_general(
-            centred, centred, (((0,), (0,)), ((), ())), precision=HIGHEST,
-            preferred_element_type=jnp.float32,
+            jnp.concatenate([high, high, low], axis=0), jnp.concatenate([high, low, high], axis=0),
+            (((0,), (0,)), ((), ())), preferred_element_type=jnp.float32,
         )
         gsend[row, 0:PATCH_CELLS, :] = diagonal_blocks(square)
         gsend[row, PATCH_CELLS:, :] = jnp.broadcast_to(mean, (TILE, lon))
@@ -257,8 +299,16 @@
         mean = gain_ref[PATCH_CELLS:PATCH_CELLS + 1, :]
         shift = gain_ref[PATCH_CELLS + 1:PATCH_CELLS + 2, :]
         half = 0.5 * (cur[row] - mean)
-        moved = jnp.dot(half, block_diagonal(gain_ref[0:PATCH_CELLS, :]), precision=HIGHEST,
-                        preferred_element_type=jnp.float32)
+        high, low = split(half)
+        gain_high, gain_low = (
+            block_diagonal(part.astype(jnp.float32)).astype(jnp.bfloat16)
+            for part in split(gain_ref[0:PATCH_CELLS, :])
+        )
+        moved = (
+            jnp.dot(high, gain_high, preferred_element_type=jnp.float32)
+            + jnp.dot(high, gain_low, preferred_element_type=jnp.float32)
+            + jnp.dot(low, gain_high, preferred_element_type=jnp.float32)
+        )
         result = half + moved + (mean + shift)
         for h in range(lon // 128):
             out_ref[pl.ds(h * rows + row, members, stride=rows * (lon // 128)), :] = result[:, h * 128:(h + 1) * 128]
@@ -281,7 +331,7 @@
 
         in_group = lax.broadcasted_iota(jnp.int32, (PATCH_CELLS, lon), 1) - groups * PATCH_CELLS
         eye = lax.broadcasted_iota(jnp.int32, (PATCH_CELLS, lon), 0) == in_group
-        inverse = invert(jnp.where(eye, 1.0, 0.0) + weight * cov, in_group)
+        inverse = invert(jnp.where(eye, 1.0, 0.0) + weight * cov)
         misfit = pull - weight * as_column(mean, eye, groups)
         push = jnp.sum(misfit * cov, axis=0, keepdims=True)
         shift = jnp.sum(as_column(push, eye, groups) * inverse, axis=0, keepdims=True)
@@ -335,9 +385,10 @@
     out = pl.pallas_call(
         functools.partial(kernel, n_mem, n_lat),
         out_shape=jax.ShapeDtypeStruct((members * rows * (lon // 128), 128), jnp.float32),
-        in_specs=[vmem, vmem, vmem, pl.BlockSpec(memory_space=pltpu.SMEM), vmem, vmem],
+        in_specs=[pl.BlockSpec(memory_space=pl.ANY), vmem, vmem, pl.BlockSpec(memory_space=pltpu.SMEM), vmem, vmem],
         out_specs=vmem,
         scratch_shapes=[
+            pltpu.VMEM((members * rows * (lon // 128), 128), jnp.float32),
             pltpu.VMEM((rows + 2 * STEPS, members, lon), jnp.float32),
             pltpu.VMEM((rows, members, lon), jnp.float32),
             pltpu.VMEM((2, rows, lon), jnp.float32),
@@ -346,6 +397,7 @@
             pltpu.VMEM((n_mem - 1, block, lon), jnp.float32),
             pltpu.VMEM((block, lon), jnp.float32),
             pltpu.VMEM((rows, block, lon), jnp.float32),
+            dma((HALO_CHUNKS,)),
             dma((2, HALO_CHUNKS)), dma((2, HALO_CHUNKS)),
             dma((2,)), dma((2,)),
             dma((n_mem - 1,)), dma((n_mem - 1,)),

time: 47.6 us -> 43.3 us (0.910)
  Pallas kernels: 45.2 us -> 40.8 us
    pallas_call x1, Pallas kernels: 45.2 us -> 40.8 us  [local(): pl.pallas_call(functools.partial(kernel, n_mem, n_lat), out_shape=jax.Sha...]
where the time goes in v2:
time: 43.3 us; the launch traced here: 43 us
  Pallas kernels  40.8 us (94%)
  local copies, waits for them, and re-layouts  2.26 us (5%)
    pallas_call x1, Pallas kernels, local(): pl.pallas_call(functools.partial(kernel, n_mem, n_lat), out_shape=jax.Sha...  40.8 us
    unnamed x1, local copies, waits for them, and re-layouts  2.26 us

profile of v2, /device:TPU:1, one launch (start us, length us, event | category | flops | bytes accessed | tf_op | source)
XLA Modules:
  0.0 43.0 jit_solution(2577873521115379586)
XLA Ops:
  0.0 40.8 %cycle.1 = f32[2048,128]{1,0:T(8,128)} custom-call(f32[2048,128]{1,0:T(8,128)} %bitcast.14, f32[8,256]{1,0:T(8,128)} %forcing_ref.1, s32[32,256]{1,0:T(8,128)} %bitcast.15, s32[1,4]{1,0:T(1,128)} %count_ref.1, f32[4,256]{1,0:T(4,128)} %bitcast.16, f32[4,256]{1,0:T(4,128)} %bitcast.17), custom_call_target="tpu_custom_call" | custom-call | tf_op jit(solution)/shard_map/cycle/pallas_call | solution.py:385
  40.8 2.3 %copy.8 = f32[128,8,256]{2,1,0:T(8,128)} copy(f32[128,8,256]{2,1,0:T(8,128)} %bitcast.13) | data formatting | bytes 2097152

commit v3 on v2

--- a/solution.py
+++ b/solution.py
@@ -11,7 +11,7 @@
 STEPS = 4
 TIME_STEP = 0.05
 LAT_MIXING = 4.0
-HALO_CHUNKS = 4
+HALO_CHUNKS = 8
 TILE = 8
 PIVOTS = 4
 
@@ -100,9 +100,9 @@
     return high, (values - high.astype(jnp.float32)).astype(jnp.bfloat16)
 
 
-def kernel(n_mem, n_lat, fields_ref, forcing_ref, cell_ref, count_ref, value_ref, var_ref, out_ref,
-           landed, ext, cur, fbuf, fwide, gsend, grecv, nsend, nrecv,
-           load_sem, halo_send, halo_recv, force_send, force_recv, gram_send, gram_recv, gain_send, gain_recv):
+def kernel(n_mem, n_lat, fields_ref, forcing_in, cell_in, count_in, value_in, var_in, out_ref,
+           forcing_ref, cell_ref, count_ref, value_ref, var_ref, landed, ext, cur, fbuf, fwide, gsend, grecv, nsend, nrecv,
+           small_sem, load_sem, halo_send, halo_recv, force_send, force_recv, gram_send, gram_recv, gain_send, gain_recv):
     rows, members, lon = cur.shape
     share = n_mem // rows
     per_row = lon // PATCH_CELLS
@@ -126,6 +126,15 @@
     def _():
         pl.semaphore_signal(barrier, inc=1, device_id={"lat": strip + 1}, device_id_type=MESH)
 
+    small = [
+        pltpu.make_async_copy(source, target, small_sem.at[i])
+        for i, (source, target) in enumerate((
+            (forcing_in, forcing_ref), (cell_in, cell_ref), (count_in, count_ref),
+            (value_in, value_ref), (var_in, var_ref),
+        ))
+    ]
+    for copy in small:
+        copy.start()
     pitch = rows * (lon // 128)
 
     def load(c):
@@ -143,6 +152,8 @@
                     pl.ds(c * chunk * pitch + h * rows + r, chunk, stride=pitch), :]
 
     rows_first(0)
+    for copy in small:
+        copy.wait()
     pl.semaphore_wait(barrier, n_mem - 1 + has_before.astype(jnp.int32) + has_after.astype(jnp.int32))
 
     def halo_copy(side, c):
@@ -385,9 +396,14 @@
     out = pl.pallas_call(
         functools.partial(kernel, n_mem, n_lat),
         out_shape=jax.ShapeDtypeStruct((members * rows * (lon // 128), 128), jnp.float32),
-        in_specs=[pl.BlockSpec(memory_space=pl.ANY), vmem, vmem, pl.BlockSpec(memory_space=pltpu.SMEM), vmem, vmem],
+        in_specs=[pl.BlockSpec(memory_space=pltpu.HBM)] * 6,
         out_specs=vmem,
         scratch_shapes=[
+            pltpu.VMEM(forcing.shape, jnp.float32),
+            pltpu.VMEM((obs_cell.shape[1], slots), jnp.int32),
+            pltpu.SMEM(obs_count.shape, jnp.int32),
+            pltpu.VMEM((per_row, slots), jnp.float32),
+            pltpu.VMEM((per_row, slots), jnp.float32),
             pltpu.VMEM((members * rows * (lon // 128), 128), jnp.float32),
             pltpu.VMEM((rows + 2 * STEPS, members, lon), jnp.float32),
             pltpu.VMEM((rows, members, lon), jnp.float32),
@@ -397,22 +413,23 @@
             pltpu.VMEM((n_mem - 1, block, lon), jnp.float32),
             pltpu.VMEM((block, lon), jnp.float32),
             pltpu.VMEM((rows, block, lon), jnp.float32),
+            dma((5,)),
             dma((HALO_CHUNKS,)),
             dma((2, HALO_CHUNKS)), dma((2, HALO_CHUNKS)),
             dma((2,)), dma((2,)),
             dma((n_mem - 1,)), dma((n_mem - 1,)),
             dma((n_mem - 1,)), dma((n_mem - 1,)),
         ],
-        compiler_params=pltpu.CompilerParams(collective_id=0, has_side_effects=True),
+        compiler_params=pltpu.CompilerParams(collective_id=0, has_side_effects=True, vmem_limit_bytes=16 * 2 ** 20),
         name="cycle",
-    )(
+    )(*(pltpu.with_memory_space_constraint(a, pltpu.HBM) for a in (
         fields.reshape(members, rows, lon // 128, 128).transpose(0, 2, 1, 3).reshape(-1, 128),
         forcing,
         obs_cell.reshape(-1, slots),
         obs_count,
         obs_value.reshape(-1, slots),
         obs_var.reshape(-1, slots),
-    )
+    )))
     return out.reshape(members, lon // 128, rows, 128).transpose(0, 2, 1, 3).reshape(members, rows, lon)
 
 

time: 43.3 us -> 39.5 us (0.912)
  Pallas kernels: 40.8 us -> 38.4 us
  local copies, waits for them, and re-layouts: 2.26 us -> 0.97 us
    pallas_call x1, Pallas kernels: 40.8 us -> 38.4 us  [local(): pl.pallas_call(functools.partial(kernel, n_mem, n_lat), out_shape=jax.Sha...]
    unnamed x1, local copies, waits for them, and re-layouts: 2.26 us -> 0.97 us
where the time goes in v3:
time: 39.5 us; the launch traced here: 39.3 us
  Pallas kernels  38.4 us (97%)
  local copies, waits for them, and re-layouts  0.97 us (2%)
    pallas_call x1, Pallas kernels, local(): pl.pallas_call(functools.partial(kernel, n_mem, n_lat), out_shape=jax.Sha...  38.4 us
    unnamed x1, local copies, waits for them, and re-layouts  0.97 us

profile of v3, /device:TPU:1, one launch (start us, length us, event | category | flops | bytes accessed | tf_op | source)
XLA Modules:
  0.0 39.3 jit_solution(12319762075611731178)
XLA Ops:
  0.0 38.4 %cycle.1 = f32[2048,128]{1,0:T(8,128)S(1)} custom-call(f32[2048,128]{1,0:T(8,128)} %bitcast.14, f32[8,256]{1,0:T(8,128)} %forcing_in.1, s32[32,256]{1,0:T(8,128)} %bitcast.15, s32[1,4]{1,0:T(1,128)} %count_in.1, f32[4,256]{1,0:T(4,128)} %bitcast.16, f32[4,256]{1,0:T(4,128)} %bitcast.17), custom_call_target="tpu_custom_call" | custom-call | tf_op jit(solution)/shard_map/cycle/pallas_call | solution.py:396
  38.4 1.0 %copy.8 = f32[128,8,256]{2,1,0:T(8,128)} copy(f32[128,8,256]{2,1,0:T(8,128)S(1)} %bitcast.13) | data formatting | bytes 2097152
